TPU v7x, 256 devices: a whole 4x4x8 slice. The times are simulated.
256 devices in a mesh: row: 32 (over z, x_lo, core), col: 8 (over y, x_hi).
Axes of the slice: x: 4 (x_hi: 2, x_lo: 2; x = x_hi * 2 + x_lo), y: 4, z: 8, core: 2. Of those that a mesh axis runs over, the one named last changes fastest.
Arguments:
- vectors: bfloat16 [8, 262144], P(None, ('row', 'col')), may hold values from -6 to 6
- energies: float32 [262144], P(('row', 'col')), may hold values from 0.5 to 6
- tiles: bfloat16 [262144, 4096], P(('row', 'col')), may hold values from -0.25 to 0.25
- tile_rows: int32 [262144], P(('row', 'col')), may hold values from 0 to 127, as said below
- tile_cols: int32 [262144], P(('row', 'col')), may hold values from 0 to 511
- tile_count: int32 [256], P(('row', 'col')), may hold values from 128 to 1024, as said below
Outputs:
- product: bfloat16 [8, 262144], P(None, ('row', 'col'))
- residual: float32 [8, 262144], P(None, ('row', 'col'))
Inputs may be any that keep to these rules, and one draw needn't show every extreme that they name: `tile_count`: every count is at least 128, and some device uses all 1024 slots in every draw; a few devices are full while most use far fewer. `tile_rows`: slots may name the same row and column block more than once; such tiles add.
All inputs are finite; a program needn't handle non-finite values.
Results may differ from a plain program's by a relative error of at most 0.008.
Values may be sent and summed in bfloat16 or wider, within the bound.
A program may use at most 64 MiB of HBM per device.

v0:
```python
import jax
import jax.numpy as jnp
from jax import lax
from jax.sharding import PartitionSpec as P


def per_device(vectors, energies, tiles, tile_rows, tile_cols, tile_count):
    kvec = vectors.shape[0]
    own_states = vectors.shape[1]
    blk_own = own_states // 64
    n_row = lax.axis_size("row")
    n_col = lax.axis_size("col")
    seg_blocks = n_col * blk_own
    slots = tiles.shape[0]
    group = min(128, slots)
    gathered = lax.all_gather(vectors, "row", axis=1, tiled=True)
    blocks = gathered.reshape(kvec, n_row * blk_own, 64)
    seg_ids = jnp.arange(seg_blocks, dtype=jnp.int32)
    group_ids = jnp.arange(group, dtype=jnp.int32)
    count = tile_count[0]
    turns = (count + group - 1) // group

    def add_group(step, accum):
        first = step * group
        tile_part = lax.dynamic_slice_in_dim(tiles, first, group, 0).reshape(group, 64, 64)
        row_part = lax.dynamic_slice_in_dim(tile_rows, first, group, 0)
        col_part = lax.dynamic_slice_in_dim(tile_cols, first, group, 0)
        picked = jnp.take(blocks, col_part, axis=1)
        prod = jnp.einsum("tji,kti->ktj", tile_part, picked, preferred_element_type=jnp.float32)
        live = first + group_ids < count
        onehot = ((row_part[:, None] == seg_ids[None, :]) & live[:, None]).astype(jnp.bfloat16)
        upper = prod.astype(jnp.bfloat16)
        lower = (prod - upper.astype(jnp.float32)).astype(jnp.bfloat16)
        added = jnp.einsum("ktj,tr->krj", upper, onehot, preferred_element_type=jnp.float32)
        added = added + jnp.einsum("ktj,tr->krj", lower, onehot, preferred_element_type=jnp.float32)
        return accum + added

    accum = jnp.zeros((kvec, seg_blocks, 64), jnp.float32)
    accum = lax.fori_loop(0, turns, add_group, accum)
    partial_value = accum.reshape(kvec, seg_blocks * 64)
    summed = lax.psum(partial_value.astype(jnp.bfloat16), "col").astype(jnp.float32)
    share = lax.dynamic_slice_in_dim(summed, lax.axis_index("col") * own_states, own_states, 1)
    vec32 = vectors.astype(jnp.float32)
    diag_part = energies[None, :] * vec32
    whole = diag_part + share
    terms = jnp.einsum("an,bn->ab", vec32, whole, precision=lax.Precision.HIGHEST)
    total_states = n_row * n_col * own_states
    gram = lax.psum(terms, ("row", "col")) / total_states
    residual = whole - jnp.einsum("ab,an->bn", gram, vec32, precision=lax.Precision.HIGHEST)
    return (whole.astype(jnp.bfloat16), residual)


def solution(mesh):
    in_specs = (
        P(None, ("row", "col")),
        P(("row", "col")),
        P(("row", "col"), None),
        P(("row", "col")),
        P(("row", "col")),
        P(("row", "col")),
    )
    out_specs = (P(None, ("row", "col")), P(None, ("row", "col")))
    return jax.shard_map(
        per_device, mesh=mesh, in_specs=in_specs, out_specs=out_specs, check_vma=False
    )
```

profile of v0, /device:TPU:1, one launch (start us, length us, event | category | flops | bytes accessed | tf_op | source)
XLA Modules:
  0.0 309.9 jit_solution(10586212366115992367)
XLA Ops:
  7.9 40.2 %all_gather.3 = bf16[8,32768]{1,0:T(8,128)(2,1)S(1)} all-gather(bf16[8,1024]{1,0:T(8,128)(2,1)} %param.8), channel_id=1, replica_groups=mesh['row'=32,'col'=8] {'row'}, dimensions={1}, use_global_device_ids=true | all-gather | bytes 540672 | tf_op jit(solution)/shard_map/all_gather | solution.py:16
  48.0 1.1 reshape.25
  49.2 1.7 copy.20
  50.9 44.8 %while.13 = (s32[]{:T(128)}, f32[8,128,64]{1,2,0:T(8,128)S(1)}, s32[]{:T(128)}, s32[1024]{0:T(1024)}, s32[]{:T(128)}, /*index=5*/s32[1024]{0:T(1024)}, bf16[8,51...) while((s32[]{:T(128)}, f32[8,128,64]{1,2,0:T(8,128)S(1)}, ...), condition=%wide.region_1.2_spmd.clone.clone, body=%wide.region_0.1_spmd.clone.clone.sunk | while | flops 42469380 | bytes 10887999 | solution.py:39
  50.9 1.3 constant_dynamic-slice_fusion.2
  52.9 2.9 copy.28
  55.8 1.4 compare_and_fusion.2
  57.2 1.9 gather_fusion
  59.1 1.2 fusion.47
  60.7 0.8 dynamic_slice.35
  62.1 1.3 constant_dynamic-slice_fusion.2
  64.1 2.9 copy.28
  67.0 1.4 compare_and_fusion.2
  68.4 1.9 gather_fusion
  70.3 1.2 fusion.47
  73.3 1.3 constant_dynamic-slice_fusion.2
  75.3 2.9 copy.28
  78.2 1.4 compare_and_fusion.2
  79.7 1.9 gather_fusion
  81.6 1.2 fusion.47
  84.5 1.3 constant_dynamic-slice_fusion.2
  86.5 2.9 copy.28
  89.4 1.4 compare_and_fusion.2
  90.9 1.9 gather_fusion
  92.8 1.2 fusion.47
  94.3 0.8 dynamic_slice.35
  95.9 0.9 convert_element_type.31
  96.9 123.3 %all-reduce.2.cloned.1.call-done = bf16[8,8192]{1,0:T(8,128)(2,1)} async-done(((bf16[8,8192]{1,0:T(8,128)(2,1)}), bf16[8,8192]{1,0:T(8,128)(2,1)}) %all-reduce.2.cloned.1.call-update) | async-done | bytes 131088 | tf_op jit(solution)/shard_map/psum | solution.py:41
  220.2 0.8 convolution_bitcast_fusion
  221.0 79.3 %psum.15 = f32[8,8]{0,1:T(8,128)S(1)} all-reduce(f32[8,8]{0,1:T(8,128)S(1)} %convolution_bitcast_fusion), channel_id=1, replica_groups=mesh['row'=32,'col'=8] {'row','col'}, use_global_device_ids=true, to_apply=%region_3.4 | all-reduce | flops 64 | bytes 512 | tf_op jit(solution)/shard_map/psum | solution.py:48
  300.3 1.3 fusion.19
  301.6 1.5 convolution_subtract_fusion
  (39 shorter events, 8.2 us)
Async XLA Ops:
  7.2 213.0 %all-reduce.2.cloned.1.call-start = ((), (), s32[]{:S(2)}) async-start(), calls=%async_computation | async-start | bytes 262144 | tf_op jit(solution)/shard_map/psum | solution.py:41
  50.8 169.3 %copy-start = (bf16[8,1024]{1,0:T(8,128)(2,1)S(1)}, bf16[8,1024]{1,0:T(8,128)(2,1)}, u32[]{:S(2)}) copy-start(bf16[8,1024]{1,0:T(8,128)(2,1)} %param.8) | copy-start | bytes 49156
  50.9 169.3 %copy-start.1 = (f32[1024]{0:T(1024)S(1)}, f32[1024]{0:T(1024)}, u32[]{:S(2)}) copy-start(f32[1024]{0:T(1024)} %param.9) | copy-start | bytes 12292
Sparse Core Ops, SparseCore 0:
  97.0 123.1 all-reduce.1
where the time goes:
time: 311 us; the launch traced here: 310 us
  waiting for transfers between devices  123 us (40%)
  blocking collectives  119 us (38%)
  local copies, waits for them, and re-layouts  35.1 us (11%)
  between operations  14.7 us (5%)
  matrix products  9.3 us (3%)
  other arithmetic  7.69 us (2%)
    psum x1, waiting for transfers between devices, per_device(): lax.psum(partial_value.astype(jnp.bfloat16), 'col').astype(jnp.float32)  123 us
    psum x1, blocking collectives, per_device(): gram = lax.psum(terms, ('row', 'col')) / total_states  79.3 us
    all_gather x1, blocking collectives, per_device(): gathered = lax.all_gather(vectors, 'row', axis=1, tiled=True)  40.2 us
    reshape x4, local copies, waits for them, and re-layouts, add_group(): lax.dynamic_slice_in_dim(tiles, first, group, 0).reshape(group, 64, 64)  11.7 us
    dynamic_slice x8, local copies, waits for them, and re-layouts, add_group(): lax.dynamic_slice_in_dim(tiles, first, group, 0).reshape(group, 64, 64)  7.96 us
    gather x4, local copies, waits for them, and re-layouts, add_group(): picked = jnp.take(blocks, col_part, axis=1)  7.58 us
  transfers between devices with their start and end apart: 1, of which 1 were waited for; matrix products, arithmetic and copies ran while one was open for 0% of the time, Pallas kernels for 0%

commit v1 on v0

v1 whole, which is shorter than its diff:
```python
import jax
import jax.numpy as jnp
from jax import lax
from jax.experimental import pallas as pl
from jax.experimental.pallas import tpu as pltpu
from jax.sharding import PartitionSpec as P

F32, BF16 = jnp.float32, jnp.bfloat16
NEAR_LAST = (4, 3, 5, 2, 6, 1, 7)
NEAR_FIRST = (1, 7, 2, 6, 3, 5, 4)


def iota(shape, dim):
    return lax.broadcasted_iota(jnp.int32, shape, dim)


def low_half():
    return iota((1, 128), 1) < 64


def turn(value):
    return pltpu.roll(value, 64, 1)


def to_blocks(natural, out_ref):
    low = low_half()
    for t in range(8):
        part = natural[:, 128 * t : 128 * t + 128]
        turned = turn(part)
        for p in range(4):
            a, b = 2 * p, 2 * p + 1
            lanes = pl.ds(128 * p, 128)
            out_ref[pl.ds(2 * t, 1), lanes] = jnp.where(low, part[a : a + 1], turned[b : b + 1])
            out_ref[pl.ds(2 * t + 1, 1), lanes] = jnp.where(low, turned[a : a + 1], part[b : b + 1])


def from_blocks(value, p, out_ref):
    low = low_half()
    turned = turn(value)
    for t in range(8):
        a, b = 2 * t, 2 * t + 1
        lanes = pl.ds(128 * t, 128)
        out_ref[pl.ds(2 * p, 1), lanes] = jnp.where(low, value[a : a + 1], turned[b : b + 1])
        out_ref[pl.ds(2 * p + 1, 1), lanes] = jnp.where(low, turned[a : a + 1], value[b : b + 1])


def onehots(rows_ref, cols_ref, count_ref, rowhot, colhot, foldhot):
    count = count_ref[0]
    slot = iota((8, 128), 0) * 128 + iota((8, 128), 1)
    rows = jnp.where(slot < count, rows_ref[...], -1)
    cols = jnp.transpose(cols_ref[...].astype(F32))
    row_ids = iota((128, 128), 0)
    col_ids = iota((128, 512), 1).astype(F32)
    for t in range(8):
        hot = row_ids == rows[t : t + 1, :]
        rowhot[:, 128 * t : 128 * t + 128] = jnp.where(hot, 1.0, 0.0).astype(BF16)
        hot = cols[:, t : t + 1] == col_ids
        colhot[t] = jnp.where(hot, 1.0, 0.0).astype(BF16)
    lane = iota((256, 128), 1)
    spot = 2 * (iota((256, 128), 0) // 8)
    for jp in range(2):
        for kp in range(2):
            hot = lane == spot + (64 * kp + jp)
            foldhot[2 * jp + kp] = jnp.where(hot, 1.0, 0.0).astype(BF16)


def products(t, colhot, picked_from, tile_ref, y_ref):
    low = low_half()
    x = jnp.dot(colhot[t], picked_from, preferred_element_type=F32)
    parts = []
    for jp in range(2):
        keep = low if jp == 0 else jnp.logical_not(low)
        for k in range(8):
            value = x[:, 128 * (k // 2) : 128 * (k // 2) + 128]
            if k % 2 != jp:
                value = turn(value)
            parts.append(jnp.where(keep, value, 0.0))
    own = iota((8, 256), 1) % 8 == iota((8, 256), 0)
    outs = []
    for g in range(16):
        left = jnp.concatenate([part[8 * g : 8 * g + 8] for part in parts], axis=0).astype(BF16)
        right = tile_ref[t, pl.ds(256 * g, 256), :]
        outs.append(
            lax.dot_general(left, right, (((1,), (1,)), ((), ())), preferred_element_type=F32)
        )
        if g % 2 == 1:
            first = pl.multiple_of(128 * t + 8 * (g - 1), 16)
            for m in range(16):
                pair = [jnp.where(own, o[8 * m : 8 * m + 8], 0.0) for o in outs]
                y_ref[m, pl.ds(first, 16), :] = jnp.concatenate(pair, axis=0).astype(BF16)
            outs = []


def scattered(p, rowhot, y_ref, foldhot):
    hots = rowhot[...]
    total = jnp.zeros((128, 128), F32)
    for jp in range(2):
        for kp in range(2):
            acc = jnp.dot(hots, y_ref[8 * jp + 2 * p + kp], preferred_element_type=F32)
            upper = acc.astype(BF16)
            lower = (acc - upper.astype(F32)).astype(BF16)
            fold = foldhot[2 * jp + kp]
            total = total + jnp.dot(upper, fold, preferred_element_type=F32)
            total = total + jnp.dot(lower, fold, preferred_element_type=F32)
    return total


def kernel(
    n_states,
    vectors_ref,
    energies_ref,
    tiles_ref,
    rows_ref,
    cols_ref,
    count_ref,
    product_ref,
    residual_ref,
    tile_vm,
    xw,
    seg,
    rowhot,
    colhot,
    foldhot,
    y_ref,
    own32,
    partial32,
    outgoing,
    incoming,
    gsum,
    stage_a,
    stage_b,
    natural,
    tile_sem,
    z_send,
    z_recv,
    x_send,
    x_recv,
    c_send,
    c_recv,
    s_send,
    s_recv,
    p_send,
    p_recv,
    a_send,
    a_recv,
    b_send,
    b_recv,
):
    row, col = lax.axis_index("row"), lax.axis_index("col")
    core, xl, z = row % 2, (row // 2) % 2, row // 4
    low = low_half()

    def row_of(z_at, xl_at, core_at):
        return (z_at * 2 + xl_at) * 2 + core_at

    def a_peer(d):
        at = (xl * 8 + col + d) % 16
        return row_of(z, at // 8, core), at % 8

    def b_peer(d):
        at = (z * 2 + core + d) % 16
        return row_of(at // 2, xl, at % 2), col

    barrier = pltpu.get_barrier_semaphore()
    for d in range(1, 16):
        for peer in (a_peer(d), b_peer(d)):
            pl.semaphore_signal(barrier, inc=1, device_id=peer, device_id_type=pl.DeviceIdType.MESH)

    def tile_copy(t):
        return pltpu.make_async_copy(tiles_ref.at[t], tile_vm.at[t], tile_sem.at[t])

    for t in range(8):
        tile_copy(t).start()

    to_blocks(vectors_ref[...].astype(F32), own32)
    xw[row] = own32[...].astype(BF16)
    seg[pl.ds(pl.multiple_of(16 * col, 16), 16), :] = own32[...].astype(BF16)

    pl.semaphore_wait(barrier, 30)

    def remote(src, dst, send, recv, peer):
        return pltpu.make_async_remote_copy(
            src_ref=src,
            dst_ref=dst,
            send_sem=send,
            recv_sem=recv,
            device_id=peer,
            device_id_type=pl.DeviceIdType.MESH,
        )

    started = []

    def send(*args):
        copy = remote(*args)
        copy.start()
        started.append(copy)

    here = (row_of(z, xl, 1 - core), col)
    across = (row_of(z, 1 - xl, core), col)
    for d in NEAR_LAST:
        peer = (row_of((z + d) % 8, xl, core), col)
        send(xw.at[row], xw.at[row], z_send.at[d], z_recv.at[d], peer)
    send(xw.at[row], xw.at[row], x_send.at[0], x_recv.at[0], across)
    send(xw.at[row], xw.at[row], c_send.at[0], c_recv.at[0], here)
    mine = seg.at[pl.ds(pl.multiple_of(16 * col, 16), 16), :]
    for d in range(1, 8):
        send(mine, mine, s_send.at[d], s_recv.at[d], (row, (col + d) % 8))

    onehots(rows_ref, cols_ref, count_ref, rowhot, colhot, foldhot)

    for d in NEAR_FIRST:
        piece = row_of((z - d) % 8, xl, core)
        remote(xw.at[piece], xw.at[piece], z_send.at[d], z_recv.at[d], across).wait_recv()
        send(xw.at[piece], xw.at[piece], x_send.at[d], x_recv.at[d], across)
        send(xw.at[piece], xw.at[piece], c_send.at[d], c_recv.at[d], here)
    for d in (0,) + NEAR_FIRST:
        piece = row_of((z - d) % 8, 1 - xl, core)
        remote(xw.at[piece], xw.at[piece], x_send.at[d], x_recv.at[d], across).wait_recv()
        send(xw.at[piece], xw.at[piece], c_send.at[8 + d], c_recv.at[8 + d], here)
    for d in range(8):
        for half in range(2):
            piece = row_of((z - d) % 8, (xl + half) % 2, 1 - core)
            at = 8 * half + d
            remote(xw.at[piece], xw.at[piece], c_send.at[at], c_recv.at[at], here).wait_recv()

    def turn_of(t, carry):
        tile_copy(t).wait()
        products(t, colhot, xw[...].reshape(512, 512), tile_vm, y_ref)
        return carry

    lax.fori_loop(0, 8, turn_of, 0)

    for p in range(4):
        total = scattered(p, rowhot, y_ref, foldhot)
        partial32[p] = total
        outgoing[:, p] = total.astype(BF16).reshape(8, 16, 128)
    for d in range(1, 8):
        peer = (row, (col + d) % 8)
        send(outgoing.at[(col + d) % 8], incoming.at[col], p_send.at[d], p_recv.at[d], peer)

    for d in range(1, 8):
        theirs = seg.at[pl.ds(pl.multiple_of(16 * ((col - d) % 8), 16), 16), :]
        remote(theirs, theirs, s_send.at[d], s_recv.at[d], here).wait_recv()

    energies = energies_ref[...]
    turned = turn(energies)
    spread = []
    for r in range(16):
        t = r // 2
        if r % 2 == 0:
            spread.append(jnp.where(low, energies[t : t + 1], turned[t : t + 1]))
        else:
            spread.append(jnp.where(low, turned[t : t + 1], energies[t : t + 1]))
    spread = jnp.concatenate(spread, axis=0)
    vec = [own32[:, 128 * p : 128 * p + 128] for p in range(4)]
    vec_turned = [turn(v) for v in vec]
    diag = [spread * v for v in vec]

    for a in range(4):
        wide = seg[:, 128 * a : 128 * a + 128].astype(F32)
        pairs = ((wide, vec[a]), (turn(wide), vec_turned[a]))
        for b in range(4):
            for kind in range(2):
                far, near = pairs[kind]
                term = (far * partial32[b]).reshape(16, 8, 128).sum(axis=0)
                term = term + (near * diag[b]).reshape(2, 8, 128).sum(axis=0)
                gsum[pl.ds(8 * a + 2 * b + kind, 1), :] = term.sum(axis=0, keepdims=True)

    lane = iota((8, 128), 1)
    sums = gsum[...]
    lows = jnp.where(low, sums, 0.0).sum(axis=1, keepdims=True)
    highs = jnp.where(low, 0.0, sums).sum(axis=1, keepdims=True)
    packed = jnp.zeros((8, 128), F32)
    for a in range(4):
        packed = jnp.where(lane == a, lows[8 * a : 8 * a + 8], packed)
        packed = jnp.where(lane == 4 + a, highs[8 * a : 8 * a + 8], packed)

    at_a, at_b = xl * 8 + col, z * 2 + core
    stage_a[at_a] = packed
    for d in range(1, 16):
        send(stage_a.at[at_a], stage_a.at[at_a], a_send.at[d], a_recv.at[d], a_peer(d))
    for d in range(1, 16):
        theirs = stage_a.at[(at_a - d) % 16]
        remote(theirs, theirs, a_send.at[d], a_recv.at[d], here).wait_recv()
    stage_b[at_b] = stage_a[...].sum(axis=0)
    for d in range(1, 16):
        send(stage_b.at[at_b], stage_b.at[at_b], b_send.at[d], b_recv.at[d], b_peer(d))

    for d in range(1, 8):
        theirs = incoming.at[(col - d) % 8]
        remote(theirs, theirs, p_send.at[d], p_recv.at[d], here).wait_recv()
    incoming[col] = jnp.zeros((4, 16, 128), BF16)
    whole = []
    for p in range(4):
        share = partial32[p, pl.ds(pl.multiple_of(16 * col, 16), 16), :]
        for c in range(8):
            share = share + incoming[c, p].astype(F32)
        whole.append(diag[p] + share)
        from_blocks(whole[p], p, natural)
    product_ref[...] = natural[...].astype(BF16)

    for d in range(1, 16):
        theirs = stage_b.at[(at_b - d) % 16]
        remote(theirs, theirs, b_send.at[d], b_recv.at[d], here).wait_recv()
    gram = stage_b[...].sum(axis=0) / n_states
    rest = list(whole)
    for a in range(4):
        coef = jnp.where(low, gram[:, a : a + 1], gram[:, 4 + a : 5 + a])
        for b in range(4):
            rest[b] = rest[b] - coef[2 * b : 2 * b + 1] * vec[a]
            rest[b] = rest[b] - coef[2 * b + 1 : 2 * b + 2] * vec_turned[a]
    for p in range(4):
        from_blocks(rest[p], p, residual_ref)

    for copy in started:
        copy.wait_send()


def per_device(vectors, energies, tiles, tile_rows, tile_cols, tile_count):
    n_states = 32 * 8 * 1024
    stored = tiles.reshape(128, 8, 32, 128).transpose(0, 2, 1, 3).reshape(8, 4096, 128)
    vmem = pl.BlockSpec(memory_space=pltpu.VMEM)
    dma = pltpu.SemaphoreType.DMA
    return pl.pallas_call(
        lambda *refs: kernel(n_states, *refs),
        out_shape=(
            jax.ShapeDtypeStruct((8, 1024), BF16),
            jax.ShapeDtypeStruct((8, 1024), F32),
        ),
        in_specs=[
            vmem,
            vmem,
            pl.BlockSpec(memory_space=pltpu.HBM),
            vmem,
            vmem,
            pl.BlockSpec(memory_space=pltpu.SMEM),
        ],
        out_specs=(vmem, vmem),
        scratch_shapes=[
            pltpu.VMEM((8, 4096, 128), BF16),
            pltpu.VMEM((32, 16, 512), BF16),
            pltpu.VMEM((128, 512), BF16),
            pltpu.VMEM((128, 1024), BF16),
            pltpu.VMEM((8, 128, 512), BF16),
            pltpu.VMEM((4, 256, 128), BF16),
            pltpu.VMEM((16, 1024, 256), BF16),
            pltpu.VMEM((16, 512), F32),
            pltpu.VMEM((4, 128, 128), F32),
            pltpu.VMEM((8, 4, 16, 128), BF16),
            pltpu.VMEM((8, 4, 16, 128), BF16),
            pltpu.VMEM((32, 128), F32),
            pltpu.VMEM((16, 8, 128), F32),
            pltpu.VMEM((16, 8, 128), F32),
            pltpu.VMEM((8, 1024), F32),
            dma((8,)),
            dma((8,)),
            dma((8,)),
            dma((8,)),
            dma((8,)),
            dma((16,)),
            dma((16,)),
            dma((8,)),
            dma((8,)),
            dma((8,)),
            dma((8,)),
            dma((16,)),
            dma((16,)),
            dma((16,)),
            dma((16,)),
        ],
        compiler_params=pltpu.CompilerParams(
            collective_id=0, has_side_effects=True, vmem_limit_bytes=48 * 2**20
        ),
    )(
        vectors,
        energies.reshape(8, 128),
        stored,
        tile_rows.reshape(8, 128),
        tile_cols.reshape(8, 128),
        tile_count,
    )


def solution(mesh):
    in_specs = (
        P(None, ("row", "col")),
        P(("row", "col")),
        P(("row", "col"), None),
        P(("row", "col")),
        P(("row", "col")),
        P(("row", "col")),
    )
    out_specs = (P(None, ("row", "col")), P(None, ("row", "col")))
    return jax.shard_map(
        per_device, mesh=mesh, in_specs=in_specs, out_specs=out_specs, check_vma=False
    )
```

time: 311 us -> 48.8 us (0.16)
  waiting for transfers between devices: 123 us -> 0 us
  blocking collectives: 119 us -> 0 us
  Pallas kernels: 0 us -> 43.2 us
  local copies, waits for them, and re-layouts: 35.1 us -> 3.99 us
  between operations: 14.7 us -> 1.3 us
  matrix products: 9.3 us -> 0 us
  other arithmetic: 7.69 us -> 0 us
    psum x1 -> x0, waiting for transfers between devices: 123 us -> none  [per_device(): lax.psum(partial_value.astype(jnp.bfloat16), 'col').astype(jnp.float32)]
    psum x1 -> x0, blocking collectives: 79.3 us -> none  [per_device(): gram = lax.psum(terms, ('row', 'col')) / total_states]
    pallas_call x0 -> x1, Pallas kernels: none -> 43.2 us  [per_device(): pl.pallas_call(lambda *refs: kernel(n_states, *refs), out_shape=(jax.Shap...]
    all_gather x1 -> x0, blocking collectives: 40.2 us -> none  [per_device(): gathered = lax.all_gather(vectors, 'row', axis=1, tiled=True)]
    reshape x5 -> x0, local copies, waits for them, and re-layouts: 12.8 us -> none  [the longest x4 11.7 us: add_group(): lax.dynamic_slice_in_dim(tiles, first, group, 0).reshape(group, 64, 64)]
    dynamic_slice x12 -> x0, local copies, waits for them, and re-layouts: 11 us -> none  [the longest x8 7.96 us: add_group(): lax.dynamic_slice_in_dim(tiles, first, group, 0).reshape(group, 64, 64)]
    gather x4 -> x0, local copies, waits for them, and re-layouts: 7.58 us -> none  [add_group(): picked = jnp.take(blocks, col_part, axis=1)]
    dot_general x6 -> x0, matrix products: 7.24 us -> none  [the longest x4 4.94 us: add_group(): jnp.einsum('tji,kti->ktj', tile_part, picked, preferred_element_type=jnp....]
  transfers between devices with their start and end apart: 1 -> 0, of which waited for: 1 -> 0; matrix products, arithmetic and copies ran while one was open for 0% -> 0% of each run, Pallas kernels for 0% -> 0%
where the time goes in v1:
time: 48.8 us; the launch traced here: 48.5 us
  Pallas kernels  43.2 us (89%)
  local copies, waits for them, and re-layouts  3.99 us (8%)
  between operations  1.3 us (3%)
    pallas_call x1, Pallas kernels, per_device(): pl.pallas_call(lambda *refs: kernel(n_states, *refs), out_shape=(jax.Shap...  43.2 us
    unnamed x10, local copies, waits for them, and re-layouts  3.99 us

profile of v1, /device:TPU:1, one launch (start us, length us, event | category | flops | bytes accessed | tf_op | source)
XLA Modules:
  0.0 48.5 jit_solution(1952875844271163492)
XLA Ops:
  1.3 0.0 copy-start
  1.3 0.7 %copy-done = bf16[8,1024]{1,0:T(8,128)(2,1)S(1)} copy-done((bf16[8,1024]{1,0:T(8,128)(2,1)S(1)}, bf16[8,1024]{1,0:T(8,128)(2,1)}, u32[]{:S(2)}) %copy-start) | copy-done | bytes 16408
  2.0 0.0 copy-start.1
  2.0 0.7 %copy-done.1 = f32[1024]{0:T(1024)S(1)} copy-done((f32[1024]{0:T(1024)S(1)}, f32[1024]{0:T(1024)}, u32[]{:S(2)}) %copy-start.1) | copy-done | bytes 4120
  2.7 0.0 copy-start.2
  2.7 0.7 %copy-done.2 = s32[1024]{0:T(1024)S(1)} copy-done((s32[1024]{0:T(1024)S(1)}, s32[1024]{0:T(1024)}, u32[]{:S(2)}) %copy-start.2) | copy-done | bytes 4120
  3.4 0.0 copy-start.3
  3.4 0.7 %copy-done.3 = s32[1024]{0:T(1024)S(1)} copy-done((s32[1024]{0:T(1024)S(1)}, s32[1024]{0:T(1024)}, u32[]{:S(2)}) %copy-start.3) | copy-done | bytes 4120
  4.1 43.2 %shard_map.77 = (bf16[8,1024]{1,0:T(8,128)(2,1)S(1)}, f32[8,1024]{1,0:T(8,128)S(1)}) custom-call(bf16[8,1024]{1,0:T(8,128)(2,1)S(1)} %copy-done, f32[8,128]{1,0:T(8,128)S(1)} %bitcast.8, bf16[8,4096,128]{2,1,0:T(8,128)(2,1)} %bitcast.11, s32[8,128]{1,0:T(8,128)S(1)} %bitcast.9, s32[8,128]{1,0:T(8,128)S(1)} %bitcast.10, s32[1]{0:T(128)S(6)} %copy.10.refs_5_), custom_call_target="tpu_custom_call" | custom-call | tf_op jit(solution)/shard_map/pallas_call | solution.py:324
  47.2 0.6 %copy.11 = bf16[8,1024]{1,0:T(8,128)(2,1)} copy(bf16[8,1024]{1,0:T(8,128)(2,1)S(1)} %get-tuple-element.4) | data formatting | bytes 32768
  47.8 0.6 %copy.12 = f32[8,1024]{1,0:T(8,128)} copy(f32[8,1024]{1,0:T(8,128)S(1)} %get-tuple-element.5) | data formatting | bytes 65536
Async XLA Ops:
  1.3 0.7 %copy-start = (bf16[8,1024]{1,0:T(8,128)(2,1)S(1)}, bf16[8,1024]{1,0:T(8,128)(2,1)}, u32[]{:S(2)}) copy-start(bf16[8,1024]{1,0:T(8,128)(2,1)} %refs_0_.1) | copy-start | bytes 49156
  2.0 0.7 %copy-start.1 = (f32[1024]{0:T(1024)S(1)}, f32[1024]{0:T(1024)}, u32[]{:S(2)}) copy-start(f32[1024]{0:T(1024)} %param.7) | copy-start | bytes 12292
  2.7 0.7 %copy-start.2 = (s32[1024]{0:T(1024)S(1)}, s32[1024]{0:T(1024)}, u32[]{:S(2)}) copy-start(s32[1024]{0:T(1024)} %param.9) | copy-start | bytes 12292
  3.4 0.7 %copy-start.3 = (s32[1024]{0:T(1024)S(1)}, s32[1024]{0:T(1024)}, u32[]{:S(2)}) copy-start(s32[1024]{0:T(1024)} %param.10) | copy-start | bytes 12292

commit v2 on v1

v2 whole, which is shorter than its diff:
```python
import jax
import jax.numpy as jnp
from jax import lax
from jax.experimental import pallas as pl
from jax.experimental.pallas import tpu as pltpu
from jax.sharding import PartitionSpec as P

F32, BF16 = jnp.float32, jnp.bfloat16


def iota(shape, dim):
    return lax.broadcasted_iota(jnp.int32, shape, dim)


def low_half():
    return iota((1, 128), 1) < 64


def turn(value):
    return pltpu.roll(value, 64, 1)


def to_blocks(natural, out_ref):
    low = low_half()
    for t in range(8):
        part = natural[:, 128 * t : 128 * t + 128]
        turned = turn(part)
        for p in range(4):
            a, b = 2 * p, 2 * p + 1
            lanes = pl.ds(128 * p, 128)
            out_ref[pl.ds(2 * t, 1), lanes] = jnp.where(low, part[a : a + 1], turned[b : b + 1])
            out_ref[pl.ds(2 * t + 1, 1), lanes] = jnp.where(low, turned[a : a + 1], part[b : b + 1])


def from_blocks(value, p, out_ref):
    low = low_half()
    turned = turn(value)
    for t in range(8):
        a, b = 2 * t, 2 * t + 1
        lanes = pl.ds(128 * t, 128)
        out_ref[pl.ds(2 * p, 1), lanes] = jnp.where(low, value[a : a + 1], turned[b : b + 1])
        out_ref[pl.ds(2 * p + 1, 1), lanes] = jnp.where(low, turned[a : a + 1], value[b : b + 1])


def mirrored(value):
    lane = iota(value.shape, 1)
    for bit in (1, 2, 4):
        swapped = jnp.where((lane & bit) != 0, pltpu.roll(value, bit, 1), pltpu.roll(value, 128 - bit, 1))
        value = swapped
    return value


def onehots(rows_ref, cols_ref, count_ref, rowhot, colhot, foldhot):
    count = count_ref[0]
    slot = iota((8, 128), 0) * 128 + iota((8, 128), 1)
    rows = mirrored(jnp.where(slot < count, rows_ref[...], -1))
    cols = jnp.transpose(mirrored(cols_ref[...]).astype(F32))
    row_ids = iota((128, 128), 0)
    col_ids = iota((128, 512), 1).astype(F32)
    for t in range(8):
        hot = row_ids == rows[t : t + 1, :]
        rowhot[:, 128 * t : 128 * t + 128] = jnp.where(hot, 1.0, 0.0).astype(BF16)
        hot = cols[:, t : t + 1] == col_ids
        colhot[128 * t : 128 * t + 128, :] = jnp.where(hot, 1.0, 0.0).astype(BF16)
    at = iota((256, 512), 0)
    spot = 64 * (at % 8) + 2 * (at // 8)
    lane = iota((256, 512), 1)
    for jp in range(2):
        foldhot[jp] = jnp.where(lane == spot + jp, 1.0, 0.0).astype(BF16)


def products(t, x_ref, tile_ref, z_ref):
    low = low_half()
    parts = []
    for jp in range(2):
        keep = low if jp == 0 else jnp.logical_not(low)
        for k in range(8):
            value = x_ref[pl.ds(pl.multiple_of(128 * t, 128), 128), 128 * (k // 2) : 128 * (k // 2) + 128]
            if k % 2 != jp:
                value = turn(value)
            parts.append(jnp.where(keep, value, 0.0))
    away = (iota((8, 128), 1) + iota((8, 128), 0) + 1) % 8
    outs = []
    for g in range(16):
        left = jnp.concatenate([part[8 * g : 8 * g + 8] for part in parts], axis=0).astype(BF16)
        right = tile_ref[t, pl.ds(256 * g, 256), :]
        out = lax.dot_general(left, right, (((1,), (1,)), ((), ())), preferred_element_type=F32)
        merged = []
        for jp in range(2):
            for h in range(2):
                lanes = slice(128 * h, 128 * h + 128)
                both = out[64 * jp : 64 * jp + 8, lanes]
                for k in range(1, 8):
                    first = 64 * jp + 8 * k
                    moved = pltpu.roll(out[first : first + 8, lanes], k, 1)
                    both = jnp.where(away == k, moved, both)
                merged.append(pltpu.roll(both, 121, 1, stride=1, stride_axis=0))
        outs.append(merged)
        if g % 2 == 1:
            first = pl.multiple_of(128 * t + 8 * (g - 1), 16)
            for jp in range(2):
                for h in range(2):
                    pair = [o[2 * jp + h] for o in outs]
                    z_ref[jp, pl.ds(first, 16), 128 * h : 128 * h + 128] = jnp.concatenate(pair, axis=0).astype(BF16)
            outs = []


def scattered(rowhot, z_ref, foldhot):
    hots = rowhot[...]
    total = None
    for jp in range(2):
        acc = jnp.dot(hots, z_ref[jp], preferred_element_type=F32)
        upper = acc.astype(BF16)
        lower = (acc - upper.astype(F32)).astype(BF16)
        for half in (upper, lower):
            term = jnp.dot(half, foldhot[jp], preferred_element_type=F32)
            total = term if total is None else total + term
    return total


def kernel(
    n_states,
    vectors_ref,
    energies_ref,
    tiles_ref,
    rows_ref,
    cols_ref,
    count_ref,
    product_ref,
    residual_ref,
    vectors_vm,
    energies_vm,
    rows_vm,
    cols_vm,
    tile_vm,
    xw,
    seg,
    rowhot,
    colhot,
    foldhot,
    x_ref,
    z_ref,
    own32,
    partial32,
    outgoing,
    incoming,
    gsum,
    stage_a,
    stage_b,
    natural,
    in_sem,
    tile_sem,
    z_recv,
    x_recv,
    send_sem,
    recv_sem,
    known,
):
    row, col = lax.axis_index("row"), lax.axis_index("col")
    core, xl, z = row % 2, (row // 2) % 2, row // 4
    xh, y = col % 2, col // 2
    low = low_half()

    def at(z_at, x_at, core_at, y_at):
        return (z_at * 2 + x_at % 2) * 2 + core_at, y_at * 2 + x_at // 2

    x = xh * 2 + xl
    z_peer = [at((z + d) % 8, x, core, y) for d in range(8)]
    x_peer = [at(z, (x + d) % 4, core, y) for d in range(4)]
    y_peer = [at(z, x, core, (y + d) % 4) for d in range(4)]
    here = at(z, x, 1 - core, y)
    across = at(z, xh * 2 + 1 - xl, core, y)
    plane_peer = [at(z, (x + d // 4) % 4, core, (y + d % 4) % 4) for d in range(16)]
    line_peer = [at((z + d // 2) % 8, x, (core + d) % 2, y) for d in range(16)]
    mesh_ids = pl.DeviceIdType.MESH

    barrier = pltpu.get_barrier_semaphore()
    near = (z_peer[2], z_peer[6], x_peer[2], y_peer[2], z_peer[1], z_peer[7])
    near = near + (x_peer[1], x_peer[3], y_peer[1], y_peer[3], here)
    for peer in near:
        pl.semaphore_signal(barrier, inc=1, device_id=peer, device_id_type=mesh_ids)

    loads = [
        pltpu.make_async_copy(src, dst, in_sem.at[i])
        for i, (src, dst) in enumerate(
            (
                (vectors_ref, vectors_vm),
                (cols_ref, cols_vm),
                (rows_ref, rows_vm),
                (energies_ref, energies_vm),
            )
        )
    ]
    for load in loads:
        load.start()

    def tile_copy(t):
        return pltpu.make_async_copy(tiles_ref.at[t], tile_vm.at[t], tile_sem.at[t])

    for t in range(8):
        tile_copy(t).start()

    mine = seg.at[pl.ds(pl.multiple_of(16 * col, 16), 16), :]
    loads[0].wait()
    to_blocks(vectors_vm[...].astype(F32), own32)
    xw[row] = own32[...].astype(BF16)
    mine[...] = own32[...].astype(BF16)

    pl.semaphore_wait(barrier, len(near))

    def remote(src, dst, send, recv, peer):
        return pltpu.make_async_remote_copy(
            src_ref=src,
            dst_ref=dst,
            send_sem=send,
            recv_sem=recv,
            device_id=peer,
            device_id_type=mesh_ids,
        )

    def arrived(ref, recv):
        remote(ref, ref, send_sem.at[0], recv, here).wait_recv()

    def sent(ref, i):
        remote(ref, ref, send_sem.at[i], recv_sem.at[i], here).wait_send()

    def pass_on(piece, recv, peer):
        remote(xw.at[piece], xw.at[piece], send_sem.at[0], recv, peer).start()

    def to_x_and_core(piece, e):
        pass_on(piece, x_recv.at[e], across)
        pass_on(piece, recv_sem.at[0], here)

    for d in (2, 6, 1, 7):
        pass_on(row, z_recv.at[8 - d], z_peer[d])
    to_x_and_core(row, 0)
    for d in range(1, 4):
        pl.semaphore_signal(known, inc=1, device_id=y_peer[d], device_id_type=mesh_ids)

    for load in loads[1:]:
        load.wait()
    onehots(rows_vm, cols_vm, count_ref, rowhot, colhot, foldhot)

    further = {1: (6, 3), 7: (2, 5), 2: (6, 4)}

    def from_z(e):
        piece = z_peer[e][0]
        arrived(xw.at[piece], z_recv.at[e])
        if e in further:
            d, there = further[e]
            pass_on(piece, z_recv.at[there], z_peer[d])
        to_x_and_core(piece, e)

    def from_x(e):
        piece = at((z + e) % 8, xh * 2 + 1 - xl, core, y)[0]
        arrived(xw.at[piece], x_recv.at[e])
        pass_on(piece, recv_sem.at[0], here)

    for e in (1, 7, 2, 6):
        from_z(e)
    for e in (0, 1, 7):
        from_x(e)
    for e in (3, 5, 4):
        from_z(e)
    for e in (2, 6, 3, 5, 4):
        from_x(e)
    pl.semaphore_wait(known, 3)
    for d in range(1, 8):
        remote(mine, mine, send_sem.at[1], recv_sem.at[1], (row, (col + d) % 8)).start()
    arrived(xw.at[pl.ds(0, 16)], recv_sem.at[0])

    x_ref[...] = jnp.dot(colhot[...], xw[...].reshape(512, 512), preferred_element_type=F32)

    def turn_of(t, carry):
        tile_copy(t).wait()
        products(t, x_ref, tile_vm, z_ref)
        return carry

    lax.fori_loop(0, 8, turn_of, 0)

    partial32[...] = scattered(rowhot, z_ref, foldhot)
    for p in range(4):
        outgoing[:, p] = partial32[:, 128 * p : 128 * p + 128].astype(BF16).reshape(8, 16, 128)
    arrived(seg.at[pl.ds(0, 112), :], recv_sem.at[1])
    for d in range(1, 8):
        to = (col + d) % 8
        remote(outgoing.at[to], incoming.at[col], send_sem.at[2], recv_sem.at[2], (row, to)).start()

    energies = energies_vm[...]
    turned = turn(energies)
    spread = []
    for r in range(16):
        t = r // 2
        if r % 2 == 0:
            spread.append(jnp.where(low, energies[t : t + 1], turned[t : t + 1]))
        else:
            spread.append(jnp.where(low, turned[t : t + 1], energies[t : t + 1]))
    spread = jnp.concatenate(spread, axis=0)
    vec = [own32[:, 128 * p : 128 * p + 128] for p in range(4)]
    vec_turned = [turn(v) for v in vec]
    diag = [spread * v for v in vec]

    for a in range(4):
        wide = seg[:, 128 * a : 128 * a + 128].astype(F32)
        pairs = ((wide, vec[a]), (turn(wide), vec_turned[a]))
        for b in range(4):
            for kind in range(2):
                far, close = pairs[kind]
                term = (far * partial32[:, 128 * b : 128 * b + 128]).reshape(16, 8, 128).sum(axis=0)
                term = term + (close * diag[b]).reshape(2, 8, 128).sum(axis=0)
                gsum[pl.ds(8 * a + 2 * b + kind, 1), :] = term.sum(axis=0, keepdims=True)

    lane = iota((8, 128), 1)
    sums = gsum[...]
    lows = jnp.where(low, sums, 0.0).sum(axis=1, keepdims=True)
    highs = jnp.where(low, 0.0, sums).sum(axis=1, keepdims=True)
    packed = jnp.zeros((8, 128), F32)
    for a in range(4):
        packed = jnp.where(lane == a, lows[8 * a : 8 * a + 8], packed)
        packed = jnp.where(lane == 4 + a, highs[8 * a : 8 * a + 8], packed)

    at_a, at_b = x * 4 + y, z * 2 + core
    stage_a[at_a] = packed
    far_first = (10, 11, 9, 14, 6, 2, 8, 15, 13, 7, 5, 3, 1, 12, 4)
    for d in far_first:
        remote(stage_a.at[at_a], stage_a.at[at_a], send_sem.at[3], recv_sem.at[3], plane_peer[d]).start()
    arrived(stage_a.at[pl.ds(0, 15)], recv_sem.at[3])
    stage_b[at_b] = stage_a[...].sum(axis=0)
    far_first = (8, 9, 6, 7, 10, 11, 4, 5, 12, 13, 2, 3, 14, 15, 1)
    for d in far_first:
        remote(stage_b.at[at_b], stage_b.at[at_b], send_sem.at[4], recv_sem.at[4], line_peer[d]).start()

    sent(xw.at[pl.ds(0, 31)], 0)
    sent(seg.at[pl.ds(0, 112), :], 1)
    sent(outgoing.at[pl.ds(0, 7)], 2)
    sent(stage_a.at[pl.ds(0, 15)], 3)

    arrived(incoming.at[pl.ds(0, 7)], recv_sem.at[2])
    incoming[col] = jnp.zeros((4, 16, 128), BF16)
    whole = []
    own_rows = pl.ds(pl.multiple_of(16 * col, 16), 16)
    for p in range(4):
        share = partial32[own_rows, 128 * p : 128 * p + 128]
        for c in range(8):
            share = share + incoming[c, p].astype(F32)
        whole.append(diag[p] + share)
        from_blocks(whole[p], p, natural)
    product_ref[...] = natural[...].astype(BF16)

    arrived(stage_b.at[pl.ds(0, 15)], recv_sem.at[4])
    gram = stage_b[...].sum(axis=0) / n_states
    rest = list(whole)
    for a in range(4):
        coef = jnp.where(low, gram[:, a : a + 1], gram[:, 4 + a : 5 + a])
        for b in range(4):
            rest[b] = rest[b] - coef[2 * b : 2 * b + 1] * vec[a]
            rest[b] = rest[b] - coef[2 * b + 1 : 2 * b + 2] * vec_turned[a]
    for p in range(4):
        from_blocks(rest[p], p, residual_ref)
    sent(stage_b.at[pl.ds(0, 15)], 4)


def per_device(vectors, energies, tiles, tile_rows, tile_cols, tile_count):
    n_states = 32 * 8 * 1024
    stored = tiles.reshape(128, 8, 32, 128).transpose(0, 2, 1, 3).reshape(8, 4096, 128)
    vmem = pl.BlockSpec(memory_space=pltpu.VMEM)
    hbm = pl.BlockSpec(memory_space=pltpu.HBM)
    dma = pltpu.SemaphoreType.DMA
    return pl.pallas_call(
        lambda *refs: kernel(n_states, *refs),
        out_shape=(
            jax.ShapeDtypeStruct((8, 1024), BF16),
            jax.ShapeDtypeStruct((8, 1024), F32),
        ),
        in_specs=[hbm, hbm, hbm, hbm, hbm, pl.BlockSpec(memory_space=pltpu.SMEM)],
        out_specs=(vmem, vmem),
        scratch_shapes=[
            pltpu.VMEM((8, 1024), BF16),
            pltpu.VMEM((8, 128), F32),
            pltpu.VMEM((8, 128), jnp.int32),
            pltpu.VMEM((8, 128), jnp.int32),
            pltpu.VMEM((8, 4096, 128), BF16),
            pltpu.VMEM((32, 16, 512), BF16),
            pltpu.VMEM((128, 512), BF16),
            pltpu.VMEM((128, 1024), BF16),
            pltpu.VMEM((1024, 512), BF16),
            pltpu.VMEM((2, 256, 512), BF16),
            pltpu.VMEM((1024, 512), F32),
            pltpu.VMEM((2, 1024, 256), BF16),
            pltpu.VMEM((16, 512), F32),
            pltpu.VMEM((128, 512), F32),
            pltpu.VMEM((8, 4, 16, 128), BF16),
            pltpu.VMEM((8, 4, 16, 128), BF16),
            pltpu.VMEM((32, 128), F32),
            pltpu.VMEM((16, 8, 128), F32),
            pltpu.VMEM((16, 8, 128), F32),
            pltpu.VMEM((8, 1024), F32),
            dma((4,)),
            dma((8,)),
            dma((8,)),
            dma((8,)),
            dma((5,)),
            dma((5,)),
            pltpu.SemaphoreType.REGULAR,
        ],
        compiler_params=pltpu.CompilerParams(
            collective_id=0, has_side_effects=True, vmem_limit_bytes=48 * 2**20
        ),
    )(
        vectors,
        energies.reshape(8, 128),
        stored,
        tile_rows.reshape(8, 128),
        tile_cols.reshape(8, 128),
        tile_count,
    )


def solution(mesh):
    in_specs = (
        P(None, ("row", "col")),
        P(("row", "col")),
        P(("row", "col"), None),
        P(("row", "col")),
        P(("row", "col")),
        P(("row", "col")),
    )
    out_specs = (P(None, ("row", "col")), P(None, ("row", "col")))
    return jax.shard_map(
        per_device, mesh=mesh, in_specs=in_specs, out_specs=out_specs, check_vma=False
    )
```

time: 48.8 us -> 43.4 us (0.89)
  Pallas kernels: 43.2 us -> 37.8 us
    pallas_call x1, Pallas kernels: 43.2 us -> 37.8 us  [per_device(): pl.pallas_call(lambda *refs: kernel(n_states, *refs), out_shape=(jax.Shap...]
where the time goes in v2:
time: 43.4 us; the launch traced here: 43.1 us
  Pallas kernels  37.8 us (87%)
  local copies, waits for them, and re-layouts  3.99 us (9%)
  between operations  1.3 us (3%)
    pallas_call x1, Pallas kernels, per_device(): pl.pallas_call(lambda *refs: kernel(n_states, *refs), out_shape=(jax.Shap...  37.8 us
    unnamed x10, local copies, waits for them, and re-layouts  3.99 us

profile of v2, /device:TPU:1, one launch (start us, length us, event | category | flops | bytes accessed | tf_op | source)
XLA Modules:
  0.0 43.1 jit_solution(12539937991297069598)
XLA Ops:
  1.3 0.0 copy-start
  1.3 0.7 %copy-done = bf16[8,1024]{1,0:T(8,128)(2,1)S(1)} copy-done((bf16[8,1024]{1,0:T(8,128)(2,1)S(1)}, bf16[8,1024]{1,0:T(8,128)(2,1)}, u32[]{:S(2)}) %copy-start) | copy-done | bytes 16408
  2.0 0.0 copy-start.1
  2.0 0.7 %copy-done.1 = f32[1024]{0:T(1024)S(1)} copy-done((f32[1024]{0:T(1024)S(1)}, f32[1024]{0:T(1024)}, u32[]{:S(2)}) %copy-start.1) | copy-done | bytes 4120
  2.7 0.0 copy-start.2
  2.7 0.7 %copy-done.2 = s32[1024]{0:T(1024)S(1)} copy-done((s32[1024]{0:T(1024)S(1)}, s32[1024]{0:T(1024)}, u32[]{:S(2)}) %copy-start.2) | copy-done | bytes 4120
  3.4 0.0 copy-start.3
  3.4 0.7 %copy-done.3 = s32[1024]{0:T(1024)S(1)} copy-done((s32[1024]{0:T(1024)S(1)}, s32[1024]{0:T(1024)}, u32[]{:S(2)}) %copy-start.3) | copy-done | bytes 4120
  4.1 37.8 %shard_map.77 = (bf16[8,1024]{1,0:T(8,128)(2,1)S(1)}, f32[8,1024]{1,0:T(8,128)S(1)}) custom-call(bf16[8,1024]{1,0:T(8,128)(2,1)S(1)} %copy-done, f32[8,128]{1,0:T(8,128)S(1)} %bitcast.8, bf16[8,4096,128]{2,1,0:T(8,128)(2,1)} %bitcast.11, s32[8,128]{1,0:T(8,128)S(1)} %bitcast.9, s32[8,128]{1,0:T(8,128)S(1)} %bitcast.10, s32[1]{0:T(128)S(6)} %copy.10.refs_5_), custom_call_target="tpu_custom_call" | custom-call | tf_op jit(solution)/shard_map/pallas_call | solution.py:369
  41.9 0.6 %copy.11 = bf16[8,1024]{1,0:T(8,128)(2,1)} copy(bf16[8,1024]{1,0:T(8,128)(2,1)S(1)} %get-tuple-element.4) | data formatting | bytes 32768
  42.5 0.6 %copy.12 = f32[8,1024]{1,0:T(8,128)} copy(f32[8,1024]{1,0:T(8,128)S(1)} %get-tuple-element.5) | data formatting | bytes 65536
Async XLA Ops:
  1.3 0.7 %copy-start = (bf16[8,1024]{1,0:T(8,128)(2,1)S(1)}, bf16[8,1024]{1,0:T(8,128)(2,1)}, u32[]{:S(2)}) copy-start(bf16[8,1024]{1,0:T(8,128)(2,1)} %refs_0_.1) | copy-start | bytes 49156
  2.0 0.7 %copy-start.1 = (f32[1024]{0:T(1024)S(1)}, f32[1024]{0:T(1024)}, u32[]{:S(2)}) copy-start(f32[1024]{0:T(1024)} %param.7) | copy-start | bytes 12292
  2.7 0.7 %copy-start.2 = (s32[1024]{0:T(1024)S(1)}, s32[1024]{0:T(1024)}, u32[]{:S(2)}) copy-start(s32[1024]{0:T(1024)} %param.9) | copy-start | bytes 12292
  3.4 0.7 %copy-start.3 = (s32[1024]{0:T(1024)S(1)}, s32[1024]{0:T(1024)}, u32[]{:S(2)}) copy-start(s32[1024]{0:T(1024)} %param.10) | copy-start | bytes 12292

commit v3 on v2

--- a/solution.py
+++ b/solution.py
@@ -75,7 +75,7 @@
     for jp in range(2):
         keep = low if jp == 0 else jnp.logical_not(low)
         for k in range(8):
-            value = x_ref[pl.ds(pl.multiple_of(128 * t, 128), 128), 128 * (k // 2) : 128 * (k // 2) + 128]
+            value = x_ref[pl.ds(128 * t, 128), 128 * (k // 2) : 128 * (k // 2) + 128]
             if k % 2 != jp:
                 value = turn(value)
             parts.append(jnp.where(keep, value, 0.0))
@@ -97,7 +97,7 @@
                 merged.append(pltpu.roll(both, 121, 1, stride=1, stride_axis=0))
         outs.append(merged)
         if g % 2 == 1:
-            first = pl.multiple_of(128 * t + 8 * (g - 1), 16)
+            first = 128 * t + 8 * (g - 1)
             for jp in range(2):
                 for h in range(2):
                     pair = [o[2 * jp + h] for o in outs]
@@ -105,17 +105,15 @@
             outs = []
 
 
-def scattered(rowhot, z_ref, foldhot):
-    hots = rowhot[...]
-    total = None
-    for jp in range(2):
-        acc = jnp.dot(hots, z_ref[jp], preferred_element_type=F32)
-        upper = acc.astype(BF16)
-        lower = (acc - upper.astype(F32)).astype(BF16)
-        for half in (upper, lower):
-            term = jnp.dot(half, foldhot[jp], preferred_element_type=F32)
-            total = term if total is None else total + term
-    return total
+def in_two(value):
+    upper = value.astype(BF16)
+    return upper, (value - upper.astype(F32)).astype(BF16)
+
+
+def group_sum(value):
+    for shift in (64, 32, 16, 8):
+        value = value + pltpu.roll(value, shift, 1)
+    return value
 
 
 def kernel(
@@ -145,6 +143,8 @@
     outgoing,
     incoming,
     gsum,
+    seg_t,
+    shares,
     stage_a,
     stage_b,
     natural,
@@ -177,8 +177,6 @@
     barrier = pltpu.get_barrier_semaphore()
     near = (z_peer[2], z_peer[6], x_peer[2], y_peer[2], z_peer[1], z_peer[7])
     near = near + (x_peer[1], x_peer[3], y_peer[1], y_peer[3], here)
-    for peer in near:
-        pl.semaphore_signal(barrier, inc=1, device_id=peer, device_id_type=mesh_ids)
 
     loads = [
         pltpu.make_async_copy(src, dst, in_sem.at[i])
@@ -191,18 +189,17 @@
             )
         )
     ]
-    for load in loads:
-        load.start()
+    loads[0].start()
+    for peer in near:
+        pl.semaphore_signal(barrier, inc=1, device_id=peer, device_id_type=mesh_ids)
 
     def tile_copy(t):
         return pltpu.make_async_copy(tiles_ref.at[t], tile_vm.at[t], tile_sem.at[t])
 
-    for t in range(8):
-        tile_copy(t).start()
-
     mine = seg.at[pl.ds(pl.multiple_of(16 * col, 16), 16), :]
     loads[0].wait()
-    to_blocks(vectors_vm[...].astype(F32), own32)
+    own = vectors_vm[...].astype(F32)
+    to_blocks(own, own32)
     xw[row] = own32[...].astype(BF16)
     mine[...] = own32[...].astype(BF16)
 
@@ -234,12 +231,31 @@
     for d in (2, 6, 1, 7):
         pass_on(row, z_recv.at[8 - d], z_peer[d])
     to_x_and_core(row, 0)
-    for d in range(1, 4):
+
+    def share(ref, recv, peer):
+        remote(ref, ref, send_sem.at[1], recv, peer).start()
+
+    share(mine, x_recv.at[8], x_peer[2])
+    for d in (2, 1, 3):
         pl.semaphore_signal(known, inc=1, device_id=y_peer[d], device_id_type=mesh_ids)
-
+        share(mine, recv_sem.at[1], y_peer[d])
+
+    for load in loads[1:]:
+        load.start()
+    for t in range(8):
+        tile_copy(t).start()
     for load in loads[1:]:
         load.wait()
     onehots(rows_vm, cols_vm, count_ref, rowhot, colhot, foldhot)
+    energies = energies_vm[...]
+    diag = [own[:, 128 * t : 128 * t + 128] * energies[t : t + 1] for t in range(8)]
+    diag = jnp.concatenate(diag, axis=1)
+    natural[...] = diag
+    upper = diag.astype(BF16).astype(F32)
+    halves = jnp.concatenate([upper, diag - upper, jnp.zeros((112, 1024), F32)], axis=0)
+    gsum[...] = lax.dot_general(
+        vectors_vm[...], halves.astype(BF16), (((1,), (1,)), ((), ())), preferred_element_type=F32
+    )
 
     further = {1: (6, 3), 7: (2, 5), 2: (6, 4)}
 
@@ -258,6 +274,10 @@
 
     for e in (1, 7, 2, 6):
         from_z(e)
+    theirs = seg.at[pl.ds(pl.multiple_of(16 * (2 * y + 1 - xh), 16), 16), :]
+    arrived(theirs, x_recv.at[8])
+    for d in (2, 1, 3):
+        share(theirs, recv_sem.at[1], y_peer[d])
     for e in (0, 1, 7):
         from_x(e)
     for e in (3, 5, 4):
@@ -265,65 +285,50 @@
     for e in (2, 6, 3, 5, 4):
         from_x(e)
     pl.semaphore_wait(known, 3)
-    for d in range(1, 8):
-        remote(mine, mine, send_sem.at[1], recv_sem.at[1], (row, (col + d) % 8)).start()
+    for t in range(8):
+        tile_copy(t).wait()
+    arrived(seg.at[pl.ds(0, 96), :], recv_sem.at[1])
+    for jp in range(2):
+        turned = lax.dot_general(
+            foldhot[jp], seg[...], (((1,), (1,)), ((), ())), preferred_element_type=F32
+        )
+        seg_t[jp] = turned.astype(BF16)
     arrived(xw.at[pl.ds(0, 16)], recv_sem.at[0])
 
     x_ref[...] = jnp.dot(colhot[...], xw[...].reshape(512, 512), preferred_element_type=F32)
-
-    def turn_of(t, carry):
-        tile_copy(t).wait()
+    for t in range(8):
         products(t, x_ref, tile_vm, z_ref)
-        return carry
-
-    lax.fori_loop(0, 8, turn_of, 0)
-
-    partial32[...] = scattered(rowhot, z_ref, foldhot)
-    for p in range(4):
-        outgoing[:, p] = partial32[:, 128 * p : 128 * p + 128].astype(BF16).reshape(8, 16, 128)
-    arrived(seg.at[pl.ds(0, 112), :], recv_sem.at[1])
-    for d in range(1, 8):
-        to = (col + d) % 8
-        remote(outgoing.at[to], incoming.at[col], send_sem.at[2], recv_sem.at[2], (row, to)).start()
-
-    energies = energies_vm[...]
-    turned = turn(energies)
-    spread = []
-    for r in range(16):
-        t = r // 2
-        if r % 2 == 0:
-            spread.append(jnp.where(low, energies[t : t + 1], turned[t : t + 1]))
-        else:
-            spread.append(jnp.where(low, turned[t : t + 1], energies[t : t + 1]))
-    spread = jnp.concatenate(spread, axis=0)
-    vec = [own32[:, 128 * p : 128 * p + 128] for p in range(4)]
-    vec_turned = [turn(v) for v in vec]
-    diag = [spread * v for v in vec]
-
-    for a in range(4):
-        wide = seg[:, 128 * a : 128 * a + 128].astype(F32)
-        pairs = ((wide, vec[a]), (turn(wide), vec_turned[a]))
-        for b in range(4):
-            for kind in range(2):
-                far, close = pairs[kind]
-                term = (far * partial32[:, 128 * b : 128 * b + 128]).reshape(16, 8, 128).sum(axis=0)
-                term = term + (close * diag[b]).reshape(2, 8, 128).sum(axis=0)
-                gsum[pl.ds(8 * a + 2 * b + kind, 1), :] = term.sum(axis=0, keepdims=True)
-
-    lane = iota((8, 128), 1)
-    sums = gsum[...]
-    lows = jnp.where(low, sums, 0.0).sum(axis=1, keepdims=True)
-    highs = jnp.where(low, 0.0, sums).sum(axis=1, keepdims=True)
-    packed = jnp.zeros((8, 128), F32)
-    for a in range(4):
-        packed = jnp.where(lane == a, lows[8 * a : 8 * a + 8], packed)
-        packed = jnp.where(lane == 4 + a, highs[8 * a : 8 * a + 8], packed)
+
+    sums = [jnp.dot(rowhot[...], z_ref[jp], preferred_element_type=F32) for jp in range(2)]
+    cross = jnp.zeros((256, 256), F32)
+    for jp in range(2):
+        for half in in_two(sums[jp]):
+            cross = cross + jnp.dot(seg_t[jp], half, preferred_element_type=F32)
+    group = iota((8, 128), 1) // 8
+    packed = gsum[...]
+    for c in range(32):
+        block = cross[8 * c : 8 * c + 8, 128 * (c // 16) : 128 * (c // 16) + 128]
+        packed = packed + jnp.where(group == c % 16, block, 0.0)
+    packed = group_sum(packed)
 
     at_a, at_b = x * 4 + y, z * 2 + core
     stage_a[at_a] = packed
     far_first = (10, 11, 9, 14, 6, 2, 8, 15, 13, 7, 5, 3, 1, 12, 4)
     for d in far_first:
         remote(stage_a.at[at_a], stage_a.at[at_a], send_sem.at[3], recv_sem.at[3], plane_peer[d]).start()
+
+    total = None
+    for jp in range(2):
+        for half in in_two(sums[jp]):
+            term = jnp.dot(half, foldhot[jp], preferred_element_type=F32)
+            total = term if total is None else total + term
+    partial32[...] = total
+    for p in range(4):
+        outgoing[:, p] = total[:, 128 * p : 128 * p + 128].astype(BF16).reshape(8, 16, 128)
+    for d in range(1, 8):
+        to = (col + d) % 8
+        remote(outgoing.at[to], incoming.at[col], send_sem.at[2], recv_sem.at[2], (row, to)).start()
+
     arrived(stage_a.at[pl.ds(0, 15)], recv_sem.at[3])
     stage_b[at_b] = stage_a[...].sum(axis=0)
     far_first = (8, 9, 6, 7, 10, 11, 4, 5, 12, 13, 2, 3, 14, 15, 1)
@@ -337,26 +342,23 @@
 
     arrived(incoming.at[pl.ds(0, 7)], recv_sem.at[2])
     incoming[col] = jnp.zeros((4, 16, 128), BF16)
-    whole = []
     own_rows = pl.ds(pl.multiple_of(16 * col, 16), 16)
     for p in range(4):
-        share = partial32[own_rows, 128 * p : 128 * p + 128]
+        share_p = partial32[own_rows, 128 * p : 128 * p + 128]
         for c in range(8):
-            share = share + incoming[c, p].astype(F32)
-        whole.append(diag[p] + share)
-        from_blocks(whole[p], p, natural)
-    product_ref[...] = natural[...].astype(BF16)
+            share_p = share_p + incoming[c, p].astype(F32)
+        from_blocks(share_p, p, shares)
+    whole = natural[...] + shares[...]
+    product_ref[...] = whole.astype(BF16)
 
     arrived(stage_b.at[pl.ds(0, 15)], recv_sem.at[4])
     gram = stage_b[...].sum(axis=0) / n_states
-    rest = list(whole)
-    for a in range(4):
-        coef = jnp.where(low, gram[:, a : a + 1], gram[:, 4 + a : 5 + a])
-        for b in range(4):
-            rest[b] = rest[b] - coef[2 * b : 2 * b + 1] * vec[a]
-            rest[b] = rest[b] - coef[2 * b + 1 : 2 * b + 2] * vec_turned[a]
-    for p in range(4):
-        from_blocks(rest[p], p, residual_ref)
+    same = iota((8, 128), 0) == iota((8, 128), 1)
+    rest = whole
+    for a in range(8):
+        coef = jnp.where(same, gram[a : a + 1], 0.0).sum(axis=1, keepdims=True)
+        rest = rest - coef * own[a : a + 1]
+    residual_ref[...] = rest
     sent(stage_b.at[pl.ds(0, 15)], 4)
 
 
@@ -391,20 +393,22 @@
             pltpu.VMEM((128, 512), F32),
             pltpu.VMEM((8, 4, 16, 128), BF16),
             pltpu.VMEM((8, 4, 16, 128), BF16),
-            pltpu.VMEM((32, 128), F32),
+            pltpu.VMEM((8, 128), F32),
+            pltpu.VMEM((2, 256, 128), BF16),
+            pltpu.VMEM((8, 1024), F32),
             pltpu.VMEM((16, 8, 128), F32),
             pltpu.VMEM((16, 8, 128), F32),
             pltpu.VMEM((8, 1024), F32),
             dma((4,)),
             dma((8,)),
             dma((8,)),
-            dma((8,)),
+            dma((9,)),
             dma((5,)),
             dma((5,)),
             pltpu.SemaphoreType.REGULAR,
         ],
         compiler_params=pltpu.CompilerParams(
-            collective_id=0, has_side_effects=True, vmem_limit_bytes=48 * 2**20
+            collective_id=0, has_side_effects=True, vmem_limit_bytes=67_043_328
         ),
     )(
         vectors,

time: 43.4 us -> 39.9 us (0.919)
  Pallas kernels: 37.8 us -> 35.6 us
  local copies, waits for them, and re-layouts: 3.99 us -> 2.7 us
    pallas_call x1, Pallas kernels: 37.8 us -> 35.6 us  [per_device(): pl.pallas_call(lambda *refs: kernel(n_states, *refs), out_shape=(jax.Shap...]
    unnamed x10 -> x2, local copies, waits for them, and re-layouts: 3.99 us -> 2.7 us
where the time goes in v3:
time: 39.9 us; the launch traced here: 39.6 us
  Pallas kernels  35.6 us (89%)
  local copies, waits for them, and re-layouts  2.7 us (7%)
  between operations  1.29 us (3%)
    pallas_call x1, Pallas kernels, per_device(): pl.pallas_call(lambda *refs: kernel(n_states, *refs), out_shape=(jax.Shap...  35.6 us
    unnamed x2, local copies, waits for them, and re-layouts  2.7 us

profile of v3, /device:TPU:1, one launch (start us, length us, event | category | flops | bytes accessed | tf_op | source)
XLA Modules:
  0.0 39.6 jit_solution(10211543966095855285)
XLA Ops:
  1.3 35.6 %shard_map.77 = (bf16[8,1024]{1,0:T(8,128)(2,1)}, f32[8,1024]{1,0:T(8,128)}) custom-call(bf16[8,1024]{1,0:T(8,128)(2,1)} %refs_0_.1, f32[8,128]{1,0:T(8,128)} %bitcast.9, bf16[8,4096,128]{2,1,0:T(8,128)(2,1)} %bitcast.8, s32[8,128]{1,0:T(8,128)} %bitcast.10, s32[8,128]{1,0:T(8,128)} %bitcast.11, s32[1]{0:T(128)S(6)} %copy.10.refs_5_), custom_call_target="tpu_custom_call" | custom-call | tf_op jit(solution)/shard_map/pallas_call | solution.py:371
  36.9 1.3 %copy.11 = bf16[8,1024]{1,0:T(8,128)(2,1)} copy(bf16[8,1024]{1,0:T(8,128)(2,1)} %get-tuple-element.4) | data formatting | bytes 32768
  38.2 1.4 %copy.12 = f32[8,1024]{1,0:T(8,128)} copy(f32[8,1024]{1,0:T(8,128)} %get-tuple-element.5) | data formatting | bytes 65536

commit v4 on v3

--- a/solution.py
+++ b/solution.py
@@ -124,8 +124,8 @@
     rows_ref,
     cols_ref,
     count_ref,
-    product_ref,
-    residual_ref,
+    whole_ref,
+    along_ref,
     vectors_vm,
     energies_vm,
     rows_vm,
@@ -349,16 +349,16 @@
             share_p = share_p + incoming[c, p].astype(F32)
         from_blocks(share_p, p, shares)
     whole = natural[...] + shares[...]
-    product_ref[...] = whole.astype(BF16)
+    whole_ref[...] = whole
 
     arrived(stage_b.at[pl.ds(0, 15)], recv_sem.at[4])
     gram = stage_b[...].sum(axis=0) / n_states
     same = iota((8, 128), 0) == iota((8, 128), 1)
-    rest = whole
+    along = jnp.zeros((8, 1024), F32)
     for a in range(8):
         coef = jnp.where(same, gram[a : a + 1], 0.0).sum(axis=1, keepdims=True)
-        rest = rest - coef * own[a : a + 1]
-    residual_ref[...] = rest
+        along = along + coef * own[a : a + 1]
+    along_ref[...] = along
     sent(stage_b.at[pl.ds(0, 15)], 4)
 
 
@@ -368,10 +368,10 @@
     vmem = pl.BlockSpec(memory_space=pltpu.VMEM)
     hbm = pl.BlockSpec(memory_space=pltpu.HBM)
     dma = pltpu.SemaphoreType.DMA
-    return pl.pallas_call(
+    whole, along = pl.pallas_call(
         lambda *refs: kernel(n_states, *refs),
         out_shape=(
-            jax.ShapeDtypeStruct((8, 1024), BF16),
+            jax.ShapeDtypeStruct((8, 1024), F32),
             jax.ShapeDtypeStruct((8, 1024), F32),
         ),
         in_specs=[hbm, hbm, hbm, hbm, hbm, pl.BlockSpec(memory_space=pltpu.SMEM)],
@@ -408,16 +408,22 @@
             pltpu.SemaphoreType.REGULAR,
         ],
         compiler_params=pltpu.CompilerParams(
-            collective_id=0, has_side_effects=True, vmem_limit_bytes=67_043_328
+            collective_id=0, has_side_effects=True, vmem_limit_bytes=48 * 2**20
         ),
     )(
-        vectors,
-        energies.reshape(8, 128),
-        stored,
-        tile_rows.reshape(8, 128),
-        tile_cols.reshape(8, 128),
+        *(
+            pltpu.with_memory_space_constraint(value, pltpu.HBM)
+            for value in (
+                vectors,
+                energies.reshape(8, 128),
+                stored,
+                tile_rows.reshape(8, 128),
+                tile_cols.reshape(8, 128),
+            )
+        ),
         tile_count,
     )
+    return whole.astype(BF16), whole - along
 
 
 def solution(mesh):

time: 39.9 us -> 37.1 us (0.930)
  local copies, waits for them, and re-layouts: 2.7 us -> 0 us
  other arithmetic: 0 us -> 0.63 us
  Pallas kernels: 35.6 us -> 35 us
    unnamed x2 -> x0, local copies, waits for them, and re-layouts: 2.7 us -> none
    pallas_call x1, Pallas kernels: 35.6 us -> 35 us  [per_device(): pl.pallas_call(lambda *refs: kernel(n_states, *refs), out_shape=(jax.Shap...]
    sub x0 -> x1, other arithmetic: none -> 0.63 us  [per_device(): return (whole.astype(BF16), whole - along)]
where the time goes in v4:
time: 37.1 us; the launch traced here: 36.9 us
  Pallas kernels  35 us (94%)
  between operations  1.29 us (3%)
  other arithmetic  0.63 us (2%)
    pallas_call x1, Pallas kernels, per_device(): pl.pallas_call(lambda *refs: kernel(n_states, *refs), out_shape=(jax.Shap...  35 us

profile of v4, /device:TPU:1, one launch (start us, length us, event | category | flops | bytes accessed | tf_op | source)
XLA Modules:
  0.0 36.9 jit_solution(12101457435229904233)
XLA Ops:
  1.3 35.0 %shard_map.77 = (f32[8,1024]{1,0:T(8,128)S(1)}, f32[8,1024]{1,0:T(8,128)S(1)}) custom-call(bf16[8,1024]{1,0:T(8,128)(2,1)} %refs_0_.1, f32[8,128]{1,0:T(8,128)} %bitcast.9, bf16[8,4096,128]{2,1,0:T(8,128)(2,1)} %bitcast.8, s32[8,128]{1,0:T(8,128)} %bitcast.10, s32[8,128]{1,0:T(8,128)} %bitcast.11, s32[1]{0:T(128)S(6)} %copy.8.refs_5_), custom_call_target="tpu_custom_call" | custom-call | tf_op jit(solution)/shard_map/pallas_call | solution.py:371
  36.3 0.6 %fusion = (f32[8,1024]{1,0:T(8,128)}, bf16[8,1024]{1,0:T(8,128)(2,1)}) fusion(f32[8,1024]{1,0:T(8,128)S(1)} %get-tuple-element.4, f32[8,1024]{1,0:T(8,128)S(1)} %get-tuple-element.5), kind=kLoop, calls=%fused_computation | loop fusion | flops 16384 | bytes 114688 | tf_op jit(solution)/shard_map/sub | solution.py:426

commit v5 on v4

--- a/solution.py
+++ b/solution.py
@@ -244,6 +244,23 @@
         load.start()
     for t in range(8):
         tile_copy(t).start()
+    further = {1: (6, 3), 7: (2, 5), 2: (6, 4)}
+
+    def from_z(e):
+        piece = z_peer[e][0]
+        arrived(xw.at[piece], z_recv.at[e])
+        if e in further:
+            d, there = further[e]
+            pass_on(piece, z_recv.at[there], z_peer[d])
+        to_x_and_core(piece, e)
+
+    def from_x(e):
+        piece = at((z + e) % 8, xh * 2 + 1 - xl, core, y)[0]
+        arrived(xw.at[piece], x_recv.at[e])
+        pass_on(piece, recv_sem.at[0], here)
+
+    for e in (1, 7, 2, 6):
+        from_z(e)
     for load in loads[1:]:
         load.wait()
     onehots(rows_vm, cols_vm, count_ref, rowhot, colhot, foldhot)
@@ -257,23 +274,6 @@
         vectors_vm[...], halves.astype(BF16), (((1,), (1,)), ((), ())), preferred_element_type=F32
     )
 
-    further = {1: (6, 3), 7: (2, 5), 2: (6, 4)}
-
-    def from_z(e):
-        piece = z_peer[e][0]
-        arrived(xw.at[piece], z_recv.at[e])
-        if e in further:
-            d, there = further[e]
-            pass_on(piece, z_recv.at[there], z_peer[d])
-        to_x_and_core(piece, e)
-
-    def from_x(e):
-        piece = at((z + e) % 8, xh * 2 + 1 - xl, core, y)[0]
-        arrived(xw.at[piece], x_recv.at[e])
-        pass_on(piece, recv_sem.at[0], here)
-
-    for e in (1, 7, 2, 6):
-        from_z(e)
     theirs = seg.at[pl.ds(pl.multiple_of(16 * (2 * y + 1 - xh), 16), 16), :]
     arrived(theirs, x_recv.at[8])
     for d in (2, 1, 3):

time: 37.1 us -> 36.3 us (0.978)
  Pallas kernels: 35 us -> 34.2 us
    pallas_call x1, Pallas kernels: 35 us -> 34.2 us  [per_device(): pl.pallas_call(lambda *refs: kernel(n_states, *refs), out_shape=(jax.Shap...]
where the time goes in v5:
time: 36.3 us; the launch traced here: 36.1 us
  Pallas kernels  34.2 us (94%)
  between operations  1.29 us (4%)
  other arithmetic  0.63 us (2%)
    pallas_call x1, Pallas kernels, per_device(): pl.pallas_call(lambda *refs: kernel(n_states, *refs), out_shape=(jax.Shap...  34.2 us

profile of v5, /device:TPU:1, one launch (start us, length us, event | category | flops | bytes accessed | tf_op | source)
XLA Modules:
  0.0 36.1 jit_solution(17813750385010834837)
XLA Ops:
  1.3 34.2 %shard_map.77 = (f32[8,1024]{1,0:T(8,128)S(1)}, f32[8,1024]{1,0:T(8,128)S(1)}) custom-call(bf16[8,1024]{1,0:T(8,128)(2,1)} %refs_0_.1, f32[8,128]{1,0:T(8,128)} %bitcast.9, bf16[8,4096,128]{2,1,0:T(8,128)(2,1)} %bitcast.8, s32[8,128]{1,0:T(8,128)} %bitcast.10, s32[8,128]{1,0:T(8,128)} %bitcast.11, s32[1]{0:T(128)S(6)} %copy.8.refs_5_), custom_call_target="tpu_custom_call" | custom-call | tf_op jit(solution)/shard_map/pallas_call | solution.py:371
  35.5 0.6 %fusion = (f32[8,1024]{1,0:T(8,128)}, bf16[8,1024]{1,0:T(8,128)(2,1)}) fusion(f32[8,1024]{1,0:T(8,128)S(1)} %get-tuple-element.4, f32[8,1024]{1,0:T(8,128)S(1)} %get-tuple-element.5), kind=kLoop, calls=%fused_computation | loop fusion | flops 16384 | bytes 114688 | tf_op jit(solution)/shard_map/sub | solution.py:426

commit v6 on v5

--- a/solution.py
+++ b/solution.py
@@ -280,9 +280,12 @@
         share(theirs, recv_sem.at[1], y_peer[d])
     for e in (0, 1, 7):
         from_x(e)
+    from_z(3)
+    from_x(2)
+    from_z(5)
+    from_x(6)
+    from_z(4)
     for e in (3, 5, 4):
-        from_z(e)
-    for e in (2, 6, 3, 5, 4):
         from_x(e)
     pl.semaphore_wait(known, 3)
     for t in range(8):

time: 36.3 us -> 36.3 us (level)
  no operation moved by 1% of the time
where the time goes in v6:
time: 36.3 us; the launch traced here: 36.1 us
  Pallas kernels  34.2 us (94%)
  between operations  1.29 us (4%)
  other arithmetic  0.63 us (2%)
    pallas_call x1, Pallas kernels, per_device(): pl.pallas_call(lambda *refs: kernel(n_states, *refs), out_shape=(jax.Shap...  34.2 us

profile of v6, /device:TPU:1, one launch (start us, length us, event | category | flops | bytes accessed | tf_op | source)
XLA Modules:
  0.0 36.1 jit_solution(9749074548331927629)
XLA Ops:
  1.3 34.2 %shard_map.77 = (f32[8,1024]{1,0:T(8,128)S(1)}, f32[8,1024]{1,0:T(8,128)S(1)}) custom-call(bf16[8,1024]{1,0:T(8,128)(2,1)} %refs_0_.1, f32[8,128]{1,0:T(8,128)} %bitcast.9, bf16[8,4096,128]{2,1,0:T(8,128)(2,1)} %bitcast.8, s32[8,128]{1,0:T(8,128)} %bitcast.10, s32[8,128]{1,0:T(8,128)} %bitcast.11, s32[1]{0:T(128)S(6)} %copy.8.refs_5_), custom_call_target="tpu_custom_call" | custom-call | tf_op jit(solution)/shard_map/pallas_call | solution.py:374
  35.5 0.6 %fusion = (f32[8,1024]{1,0:T(8,128)}, bf16[8,1024]{1,0:T(8,128)(2,1)}) fusion(f32[8,1024]{1,0:T(8,128)S(1)} %get-tuple-element.4, f32[8,1024]{1,0:T(8,128)S(1)} %get-tuple-element.5), kind=kLoop, calls=%fused_computation | loop fusion | flops 16384 | bytes 114688 | tf_op jit(solution)/shard_map/sub | solution.py:429
